TPU v7x, 32 devices: a whole 2x2x4 slice. The times are simulated.
32 devices in a mesh: cluster: 2 (over x), sub: 16 (over z, y, core).
Axes of the slice: x: 2, y: 2, z: 4, core: 2. Of those that a mesh axis runs over, the one named last changes fastest.
Arguments:
- load_terms: float32 [32, 128, 1536], P(('cluster', 'sub')), may hold values from -60 to 60
- dual_operator: bfloat16 [32, 1536, 1536], P(('cluster', 'sub')), may hold values from -2 to 16, as said below
- dirichlet: bfloat16 [32, 1536, 1536], P(('cluster', 'sub')), may hold values from -2 to 16, as said below
- corner_coupling: bfloat16 [32, 1536, 24], P(('cluster', 'sub')), may hold values from -0.25 to 0.25
- coarse_inverse: float32 [96, 96], P(('cluster', 'sub')), may hold values from -2 to 4, as said below
- face_map: int32 [32, 6, 256], P(('cluster', 'sub')), may hold values from 0 to 255, as said below
- face_live: int32 [32, 6], P(('cluster', 'sub')), may hold values from 0 to 1, as said below
- corner_ids: int32 [32, 8], P(('cluster', 'sub')), may hold values from 0 to 31, as said below
Outputs:
- multipliers: float32 [32, 128, 1536], P(('cluster', 'sub'))
- residual: float32 [32, 128, 1536], P(('cluster', 'sub'))
Inputs may be any that keep to these rules, and one draw needn't show every extreme that they name: face_map[d, f] is a permutation of the slots of a face; the maps of the two sides of a face pair are inverse to each other. `face_live`: equal on the two sides of a face pair. `corner_ids`: the eight corners of a subdomain are the lattice vertices (c + a, s + b + 4 * e) for a, b, e in 0 and 1, taken modulo 2 and 16; each vertex has one number and is shared by eight subdomains. `dual_operator`: each subdomain's matrix is symmetric and positive definite. `dirichlet`: each subdomain's matrix is symmetric and positive definite. `coarse_inverse`: symmetric and positive definite.
All inputs are finite; a program needn't handle non-finite values.
Results may differ from a plain program's by a relative error of at most 0.0099.
Values sent between devices are 32-bit elements; how exact they have to be, the bound alone decides.
No kernel may reach another device: no remote copies, remote signals or barrier semaphores. Data moves between devices by JAX's collectives and lax.ppermute only.
A program may use at most 128 MiB of HBM per device.

v0:
```python
import jax
import jax.numpy as jnp
from jax import lax
from jax.sharding import PartitionSpec as P

ITERS = 2
STRIDE = 4


def padded(block, sides, width):
    for axis, dim in sides:
        count = lax.axis_size(axis)
        forward = [(i, i + 1) for i in range(count - 1)]
        forward.append((count - 1, 0))
        backward = [(target, source) for source, target in forward]
        low = lax.ppermute(
            lax.slice_in_dim(block, block.shape[dim] - width, None, axis=dim), axis, forward
        )
        high = lax.ppermute(lax.slice_in_dim(block, 0, width, axis=dim), axis, backward)
        block = jnp.concatenate([low, block, high], axis=dim)
    return block


def passed_along(value, axis, steps):
    count = lax.axis_size(axis)
    pairs = [(source, (source + steps) % count) for source in range(count)]
    return lax.ppermute(value, axis, pairs)


def local(
    load_terms,
    dual_operator,
    dirichlet,
    corner_coupling,
    coarse_inverse,
    face_map,
    face_live,
    corner_ids,
):
    local_loads = load_terms[0]
    operator_local = dual_operator[0]
    precond_local = dirichlet[0]
    coupling = corner_coupling[0]
    slot_maps = face_map[0]
    live_faces = face_live[0].astype(jnp.float32)
    corners = corner_ids[0]
    load_count = local_loads.shape[0]
    dual_size = local_loads.shape[1]
    face_size = dual_size // 6
    coarse_size = coarse_inverse.shape[1]
    coarse_index = (3 * corners[:, None] + jnp.arange(3, dtype=jnp.int32)[None, :]).reshape(-1)
    spread = (coarse_index[:, None] == jnp.arange(coarse_size, dtype=jnp.int32)[None, :]).astype(
        jnp.float32
    )

    def assemble(local_sum):
        face_parts = local_sum.reshape(load_count, 6, face_size)
        slab_pair = padded(jnp.stack([face_parts[:, 0], face_parts[:, 1]]), (("cluster", 0),), 1)
        row_pair = padded(jnp.stack([face_parts[:, 2], face_parts[:, 3]]), (("sub", 0),), 1)
        column_pair = []
        for source_face, shift_step in ((5, STRIDE), (4, -STRIDE)):
            column_pair.append(passed_along(face_parts[:, source_face], "sub", shift_step))
        received = [
            slab_pair[0],
            slab_pair[3],
            row_pair[0],
            row_pair[3],
            column_pair[0],
            column_pair[1],
        ]
        pieces = []
        for face_index in range(6):
            permuted = jnp.take(received[face_index], slot_maps[face_index], axis=1)
            pieces.append((face_parts[:, face_index] + permuted) * live_faces[face_index])
        return jnp.concatenate(pieces, axis=1)

    def precond_with_product(vector):
        local_term = jnp.dot(
            vector.astype(jnp.bfloat16), precond_local, preferred_element_type=jnp.float32
        )
        precond = assemble(local_term)
        product = 0.5 * lax.psum(jnp.sum(vector * precond, axis=1), ("cluster", "sub"))
        return (precond, product)

    right_side = assemble(local_loads)
    multipliers = jnp.zeros_like(right_side)
    residual = right_side
    precond, residual_dot = precond_with_product(residual)
    direction = precond
    for iteration in range(ITERS):
        rounded = direction.astype(jnp.bfloat16)
        direct = jnp.dot(rounded, operator_local, preferred_element_type=jnp.float32)
        corner_terms = jnp.dot(rounded, coupling, preferred_element_type=jnp.float32)
        coarse_local = jnp.dot(corner_terms, spread, precision=lax.Precision.HIGHEST)
        local_curve = jnp.sum(direction * direct, axis=1)
        apply_coarse_load, curve_total = lax.psum((coarse_local, local_curve), ("cluster", "sub"))
        own_values = jnp.dot(apply_coarse_load, coarse_inverse.T, precision=lax.Precision.HIGHEST)
        solution = lax.all_gather(own_values, ("cluster", "sub"), axis=1, tiled=True)
        corner_values = jnp.dot(solution, spread.T, precision=lax.Precision.HIGHEST).astype(
            jnp.bfloat16
        )
        back = lax.dot_general(
            corner_values, coupling, (((1,), (1,)), ((), ())), preferred_element_type=jnp.float32
        )
        dual_image = assemble(direct + back)
        curvature = curve_total + jnp.sum(apply_coarse_load * solution, axis=1)
        dual_image, curvature = (dual_image, curvature)
        step_size = residual_dot / curvature
        multipliers = multipliers + step_size[:, None] * direction
        residual = residual - step_size[:, None] * dual_image
        if iteration + 1 < ITERS:
            precond, residual_new = precond_with_product(residual)
            direction = precond + (residual_new / residual_dot)[:, None] * direction
            residual_dot = residual_new
    return (multipliers[None], residual[None])


def solution(mesh):
    placed = (
        P(("cluster", "sub"), None, None),
        P(("cluster", "sub"), None, None),
        P(("cluster", "sub"), None, None),
        P(("cluster", "sub"), None, None),
        P(("cluster", "sub"), None),
        P(("cluster", "sub"), None, None),
        P(("cluster", "sub"), None),
        P(("cluster", "sub"), None),
    )
    return jax.shard_map(
        local,
        mesh=mesh,
        in_specs=placed,
        out_specs=(P(("cluster", "sub"), None, None), P(("cluster", "sub"), None, None)),
        check_vma=False,
    )
```

profile of v0, /device:TPU:0, one launch (start us, length us, event | category | flops | bytes accessed | tf_op | source)
XLA Modules:
  0.0 432.1 jit_solution(1258101771140866283)
XLA Ops:
  0.7 1.4 copy.154
  2.3 3.0 collective-permute-start
  5.8 4.5 %collective-permute-start.3 = (f32[1,128,256]{2,1,0:T(8,128)S(1)}, f32[1,128,256]{2,1,0:T(8,128)S(1)}, u32[]{:S(2)}, u32[]{:S(2)}) collective-permute-start(f32[1,128,256]{2,1,0:T(8,128)S(1)} %bitcast.561), channel_id=1, source_target_pairs={{1,0},{2,1},{3,2},{4,3},{5,4},{6,5},{7,6},{8,7},{9,8},{10,9},{11,1... | collective-permute-start | bytes 393224 | tf_op jit(solution)/shard_map/ppermute | solution.py:19
  12.5 3.6 collective-permute-start.5
  16.1 6.6 %copy.173 = bf16[1,1536,1536]{1,2,0:T(8,128)(2,1)} copy(bf16[1,1536,1536]{2,1,0:T(8,128)(2,1)} %param.12) | data formatting | bytes 9437184 | tf_op args[2]
  33.2 4.0 fusion.6
  37.3 2.1 collective-permute-start.6
  39.4 4.4 %collective-permute-start.9 = (f32[1,128,256]{2,1,0:T(8,128)S(1)}, f32[1,128,256]{2,1,0:T(8,128)S(1)}, u32[]{:S(2)}, u32[]{:S(2)}) collective-permute-start(f32[1,128,256]{2,1,0:T(8,128)S(1)} %get-tuple-element.30), channel_id=1, source_target_pairs={{1,0},{2,1},{3,2},{4,3},{5,4},{6,5},{7,6},{8,7},{9,8},{10,9},{11,1... | collective-permute-start | bytes 393224 | tf_op jit(solution)/shard_map/ppermute | solution.py:19
  44.0 3.9 collective-permute-start.11
  54.3 1.3 gather_fusion.11
  60.1 3.8 multiply_reduce_fusion.3
  65.1 37.5 %all-reduce.1 = (f32[128,96]{0,1:T(8,128)S(1)}, f32[128]{0:T(128)}, f32[128]{0:T(128)}) all-reduce(f32[128,96]{0,1:T(8,128)} %fusion.53, f32[128]{0:T(128)} %get-tuple-element.4, f32[128]{0:T(128)} %get-tuple-element.3), channel_id=1, replica_groups=mesh['cluster'=2,'sub'=16] {'cluster','sub'}, use_global_device_ids=true, to_apply=%region_4.6 | all-reduce | flops 12544 | bytes 100352 | tf_op jit(solution)/shard_map/psum | solution.py:96
  103.4 41.8 %all-gather = f32[32,3,128]{2,1,0:T(4,128)S(1)} all-gather(f32[1,3,128]{2,1,0:T(4,128)S(1)} %convolution_bitcast_fusion.1), channel_id=1, replica_groups=mesh['cluster'=2,'sub'=16] {'cluster','sub'}, dimensions={0}, use_global_device_ids=true | all-gather | bytes 50688 | tf_op jit(solution)/shard_map/all_gather | solution.py:98
  147.9 1.4 copy.186
  152.3 2.0 collective-permute-start.13
  155.5 4.5 %collective-permute-start.15 = (f32[1,128,256]{2,1,0:T(8,128)S(1)}, f32[1,128,256]{2,1,0:T(8,128)}, u32[]{:S(2)}, u32[]{:S(2)}) collective-permute-start(f32[1,128,256]{2,1,0:T(8,128)S(1)} %bitcast.568), channel_id=1, source_target_pairs={{1,0},{2,1},{3,2},{4,3},{5,4},{6,5},{7,6},{8,7},{9,8},{10,9},{11,1... | collective-permute-start | bytes 393224 | tf_op jit(solution)/shard_map/ppermute | solution.py:19
  162.1 4.0 collective-permute-start.17
  167.2 1.3 gather_fusion.12
  168.5 1.7 copy.190
  172.5 1.7 copy.192
  175.2 1.3 gather_fusion.14
  176.6 1.7 copy.196
  180.6 1.7 copy.198
  185.6 2.3 constant_dynamic-update-slice_fusion.17
  188.9 1.3 gather_fusion.17
  191.3 2.2 constant_dynamic-update-slice_fusion.16
  193.5 2.3 constant_dynamic-update-slice_fusion.15
  195.7 2.1 constant_dynamic-update-slice_fusion.14
  199.2 1.4 constant_dynamic-update-slice_fusion.12
  200.6 4.3 fusion.4
  205.8 1.9 collective-permute-start.19
  207.7 4.4 %collective-permute-start.21 = (f32[1,128,256]{2,1,0:T(8,128)}, f32[1,128,256]{2,1,0:T(8,128)}, u32[]{:S(2)}, u32[]{:S(2)}) collective-permute-start(f32[1,128,256]{2,1,0:T(8,128)} %get-tuple-element.18), channel_id=1, source_target_pairs={{1,0},{2,1},{3,2},{4,3},{5,4},{6,5},{7,6},{8,7},{9,8},{10,9},{11,1... | collective-permute-start | bytes 393224 | tf_op jit(solution)/shard_map/ppermute | solution.py:19
  212.2 3.8 collective-permute-start.23
  217.0 1.4 gather_fusion.18
  218.4 1.7 copy.206
  221.0 1.3 gather_fusion.19
  222.4 1.7 copy.208
  226.4 1.7 copy.210
  230.4 1.7 copy.212
  234.4 1.7 copy.214
  236.1 2.2 constant_dynamic-update-slice_fusion.23
  241.6 2.2 constant_dynamic-update-slice_fusion.22
  243.8 2.2 constant_dynamic-update-slice_fusion.21
  246.1 2.1 constant_dynamic-update-slice_fusion.20
  248.2 2.2 constant_dynamic-update-slice_fusion.19
  250.4 1.4 constant_dynamic-update-slice_fusion.18
  251.8 1.7 multiply_reduce_fusion.1
  253.5 36.9 %psum.45 = f32[128]{0:T(128)S(1)} all-reduce(f32[128]{0:T(128)S(1)} %multiply_reduce_fusion.1), channel_id=1, replica_groups=mesh['cluster'=2,'sub'=16] {'cluster','sub'}, use_global_device_ids=true, to_apply=%region_7.9 | all-reduce | flops 128 | bytes 1024 | tf_op jit(solution)/shard_map/psum | solution.py:82
  290.9 1.4 fusion.10
  292.4 4.3 multiply_reduce_fusion
  297.0 41.7 %all-reduce = (f32[128]{0:T(128)}, f32[128,96]{0,1:T(8,128)S(1)}) all-reduce(f32[128]{0:T(128)} %get-tuple-element.85, f32[128,96]{0,1:T(8,128)S(1)} %fusion.52), channel_id=1, replica_groups=mesh['cluster'=2,'sub'=16] {'cluster','sub'}, use_global_device_ids=true, to_apply=%region_9.11 | all-reduce | flops 12416 | bytes 99328 | tf_op jit(solution)/shard_map/psum | solution.py:96
  338.8 41.1 %all-gather.1 = f32[32,3,128]{2,1,0:T(4,128)S(1)} all-gather(f32[1,3,128]{2,1,0:T(4,128)S(1)} %convolution_bitcast_fusion), channel_id=1, replica_groups=mesh['cluster'=2,'sub'=16] {'cluster','sub'}, dimensions={0}, use_global_device_ids=true | all-gather | bytes 50688 | tf_op jit(solution)/shard_map/all_gather | solution.py:98
  384.5 1.9 collective-permute-start.25
  388.5 4.5 %collective-permute-start.27 = (f32[1,128,256]{2,1,0:T(8,128)S(1)}, f32[1,128,256]{2,1,0:T(8,128)}, u32[]{:S(2)}, u32[]{:S(2)}) collective-permute-start(f32[1,128,256]{2,1,0:T(8,128)S(1)} %bitcast.573), channel_id=1, source_target_pairs={{1,0},{2,1},{3,2},{4,3},{5,4},{6,5},{7,6},{8,7},{9,8},{10,9},{11,1... | collective-permute-start | bytes 393224 | tf_op jit(solution)/shard_map/ppermute | solution.py:19
  395.5 3.8 collective-permute-start.29
  400.3 1.5 bitcast_dynamic-update-slice_fusion.11
  413.0 1.4 gather_fusion.29
  414.4 1.7 copy.235
  416.1 2.8 bitcast_dynamic-update-slice_fusion.10
  418.9 2.7 bitcast_dynamic-update-slice_fusion.9
  421.7 2.6 bitcast_dynamic-update-slice_fusion.8
  424.3 2.4 bitcast_dynamic-update-slice_fusion.7
  426.8 1.5 bitcast_dynamic-update-slice_fusion.6
  428.3 3.8 multiply_subtract_fusion
  (357 shorter events, 83.4 us)
Async XLA Ops:
  0.6 63.3 %copy-start = (bf16[1,1536,24]{1,2,0:T(8,128)(2,1)S(1)}, bf16[1,1536,24]{1,2,0:T(8,128)(2,1)}, u32[]{:S(2)}) copy-start(bf16[1,1536,24]{1,2,0:T(8,128)(2,1)} %param.13) | copy-start | bytes 221188
  2.3 27.6 %copy-start.7 = (f32[128,1,256]{2,0,1:T(8,128)}, f32[128,1,256]{2,0,1:T(8,128)S(1)}, u32[]{:S(2)}) copy-start(f32[128,1,256]{2,0,1:T(8,128)S(1)} %copy.237) | copy-start | bytes 393220
  2.3 10.2 %collective-permute-start = (f32[1,128,256]{2,1,0:T(8,128)S(1)}, f32[1,128,256]{2,1,0:T(8,128)S(1)}, u32[]{:S(2)}, u32[]{:S(2)}) collective-permute-start(f32[1,128,256]{2,1,0:T(8,128)S(1)} %bitcast.563), channel_id=1, source_target_pairs={{0,16},{16,0},{1,17},{17,1},{2,18},{18,2},{3,19},{19,3},{4,20},{20... | collective-permute-start | bytes 393224 | tf_op jit(solution)/shard_map/ppermute | solution.py:16
  5.4 23.7 %copy-start.13 = (f32[128,1,256]{2,0,1:T(8,128)}, f32[128,1,256]{2,0,1:T(8,128)S(1)}, u32[]{:S(2)}) copy-start(f32[128,1,256]{2,0,1:T(8,128)S(1)} %copy.236) | copy-start | bytes 393220
  5.4 18.9 %collective-permute-start.1 = (f32[1,128,256]{2,1,0:T(8,128)S(1)}, f32[1,128,256]{2,1,0:T(8,128)S(1)}, u32[]{:S(2)}, u32[]{:S(2)}) collective-permute-start(f32[1,128,256]{2,1,0:T(8,128)S(1)} %bitcast.564), channel_id=1, source_target_pairs={{16,0},{0,16},{17,1},{1,17},{18,2},{2,18},{19,3},{3,19},{20,4},{4,... | collective-permute-start | bytes 393224 | tf_op jit(solution)/shard_map/ppermute | solution.py:19
  5.6 25.6 %copy-start.1 = (f32[128,1,256]{2,0,1:T(8,128)}, f32[128,1,256]{2,0,1:T(8,128)S(1)}, u32[]{:S(2)}) copy-start(f32[128,1,256]{2,0,1:T(8,128)S(1)} %copy.239) | copy-start | bytes 393220
  5.6 19.7 %collective-permute-start.2 = (f32[1,128,256]{2,1,0:T(8,128)S(1)}, f32[1,128,256]{2,1,0:T(8,128)S(1)}, u32[]{:S(2)}, u32[]{:S(2)}) collective-permute-start(f32[1,128,256]{2,1,0:T(8,128)S(1)} %bitcast.560), channel_id=1, source_target_pairs={{0,1},{1,2},{2,3},{3,4},{4,5},{5,6},{6,7},{7,8},{8,9},{9,10},{10,1... | collective-permute-start | bytes 393224 | tf_op jit(solution)/shard_map/ppermute | solution.py:16
  5.8 24.7 %copy-start.3 = (f32[128,1,256]{2,0,1:T(8,128)}, f32[128,1,256]{2,0,1:T(8,128)S(1)}, u32[]{:S(2)}) copy-start(f32[128,1,256]{2,0,1:T(8,128)S(1)} %copy.238) | copy-start | bytes 393220
  5.8 20.5 %collective-permute-start.3 = (f32[1,128,256]{2,1,0:T(8,128)S(1)}, f32[1,128,256]{2,1,0:T(8,128)S(1)}, u32[]{:S(2)}, u32[]{:S(2)}) collective-permute-start(f32[1,128,256]{2,1,0:T(8,128)S(1)} %bitcast.561), channel_id=1, source_target_pairs={{1,0},{2,1},{3,2},{4,3},{5,4},{6,5},{7,6},{8,7},{9,8},{10,9},{11,1... | collective-permute-start | bytes 393224 | tf_op jit(solution)/shard_map/ppermute | solution.py:19
  10.4 16.9 %collective-permute-start.4 = (f32[128,256]{1,0:T(8,128)S(1)}, f32[128,256]{1,0:T(8,128)S(1)}, u32[]{:S(2)}, u32[]{:S(2)}) collective-permute-start(f32[128,256]{1,0:T(8,128)S(1)} %bitcast.559), channel_id=1, source_target_pairs={{0,4},{1,5},{2,6},{3,7},{4,8},{5,9},{6,10},{7,11},{8,12},{9,13},{1... | collective-permute-start | bytes 393224 | tf_op jit(solution)/shard_map/ppermute | solution.py:27
  11.5 41.2 %copy-start.70 = (pred[256]{0:T(512)(128)(4,1)}, pred[256]{0:T(512)(128)(4,1)S(1)}, u32[]{:S(2)}) copy-start(pred[256]{0:T(512)(128)(4,1)S(1)} %compare_and_fusion.5) | copy-start | bytes 772
  11.5 45.2 %copy-start.68 = (pred[256]{0:T(512)(128)(4,1)}, pred[256]{0:T(512)(128)(4,1)S(1)}, u32[]{:S(2)}) copy-start(pred[256]{0:T(512)(128)(4,1)S(1)} %compare_and_fusion.4) | copy-start | bytes 772
  11.6 45.8 %copy-start.66 = (pred[256]{0:T(512)(128)(4,1)}, pred[256]{0:T(512)(128)(4,1)S(1)}, u32[]{:S(2)}) copy-start(pred[256]{0:T(512)(128)(4,1)S(1)} %compare_and_fusion.3) | copy-start | bytes 772
  11.6 46.5 %copy-start.64 = (pred[256]{0:T(512)(128)(4,1)}, pred[256]{0:T(512)(128)(4,1)S(1)}, u32[]{:S(2)}) copy-start(pred[256]{0:T(512)(128)(4,1)S(1)} %compare_and_fusion.2) | copy-start | bytes 772
  11.6 47.0 %copy-start.62 = (pred[256]{0:T(512)(128)(4,1)}, pred[256]{0:T(512)(128)(4,1)S(1)}, u32[]{:S(2)}) copy-start(pred[256]{0:T(512)(128)(4,1)S(1)} %compare_and_fusion.1) | copy-start | bytes 772
  11.7 47.7 %copy-start.60 = (pred[256]{0:T(512)(128)(4,1)}, pred[256]{0:T(512)(128)(4,1)S(1)}, u32[]{:S(2)}) copy-start(pred[256]{0:T(512)(128)(4,1)S(1)} %compare_and_fusion) | copy-start | bytes 772
  12.5 19.3 %copy-start.5 = (f32[128,1,256]{2,0,1:T(8,128)}, f32[128,1,256]{2,0,1:T(8,128)S(1)}, u32[]{:S(2)}) copy-start(f32[128,1,256]{2,0,1:T(8,128)S(1)} %copy.240) | copy-start | bytes 393220
  12.5 15.7 %collective-permute-start.5 = (f32[128,256]{1,0:T(8,128)S(1)}, f32[128,256]{1,0:T(8,128)S(1)}, u32[]{:S(2)}, u32[]{:S(2)}) collective-permute-start(f32[128,256]{1,0:T(8,128)S(1)} %bitcast.562), channel_id=1, source_target_pairs={{0,12},{1,13},{2,14},{3,15},{4,0},{5,1},{6,2},{7,3},{8,4},{9,5},{1... | collective-permute-start | bytes 393224 | tf_op jit(solution)/shard_map/ppermute | solution.py:27
  37.3 6.8 %collective-permute-start.6 = (f32[1,128,256]{2,1,0:T(8,128)S(1)}, f32[1,128,256]{2,1,0:T(8,128)S(1)}, u32[]{:S(2)}, u32[]{:S(2)}) collective-permute-start(f32[1,128,256]{2,1,0:T(8,128)S(1)} %get-tuple-element.33), channel_id=1, source_target_pairs={{0,16},{16,0},{1,17},{17,1},{2,18},{18,2},{3,19},{19,3},{4,20},{20... | collective-permute-start | bytes 393224 | tf_op jit(solution)/shard_map/ppermute | solution.py:16
  39.3 9.5 %collective-permute-start.7 = (f32[1,128,256]{2,1,0:T(8,128)S(1)}, f32[1,128,256]{2,1,0:T(8,128)S(1)}, u32[]{:S(2)}, u32[]{:S(2)}) collective-permute-start(f32[1,128,256]{2,1,0:T(8,128)S(1)} %get-tuple-element.29), channel_id=1, source_target_pairs={{16,0},{0,16},{17,1},{1,17},{18,2},{2,18},{19,3},{3,19},{20,4},{4,... | collective-permute-start | bytes 393224 | tf_op jit(solution)/shard_map/ppermute | solution.py:19
  39.4 10.4 %collective-permute-start.8 = (f32[1,128,256]{2,1,0:T(8,128)S(1)}, f32[1,128,256]{2,1,0:T(8,128)S(1)}, u32[]{:S(2)}, u32[]{:S(2)}) collective-permute-start(f32[1,128,256]{2,1,0:T(8,128)S(1)} %get-tuple-element.32), channel_id=1, source_target_pairs={{0,1},{1,2},{2,3},{3,4},{4,5},{5,6},{6,7},{7,8},{8,9},{9,10},{10,1... | collective-permute-start | bytes 393224 | tf_op jit(solution)/shard_map/ppermute | solution.py:16
  39.4 11.3 %collective-permute-start.9 = (f32[1,128,256]{2,1,0:T(8,128)S(1)}, f32[1,128,256]{2,1,0:T(8,128)S(1)}, u32[]{:S(2)}, u32[]{:S(2)}) collective-permute-start(f32[1,128,256]{2,1,0:T(8,128)S(1)} %get-tuple-element.30), channel_id=1, source_target_pairs={{1,0},{2,1},{3,2},{4,3},{5,4},{6,5},{7,6},{8,7},{9,8},{10,9},{11,1... | collective-permute-start | bytes 393224 | tf_op jit(solution)/shard_map/ppermute | solution.py:19
  43.9 7.8 %collective-permute-start.10 = (f32[128,256]{1,0:T(8,128)S(1)}, f32[128,256]{1,0:T(8,128)S(1)}, u32[]{:S(2)}, u32[]{:S(2)}) collective-permute-start(f32[128,256]{1,0:T(8,128)S(1)} %get-tuple-element.31), channel_id=1, source_target_pairs={{0,4},{1,5},{2,6},{3,7},{4,8},{5,9},{6,10},{7,11},{8,12},{9,13},{1... | collective-permute-start | bytes 393224 | tf_op jit(solution)/shard_map/ppermute | solution.py:27
  44.0 20.1 %copy-start.74 = (s32[24]{0:T(128)}, s32[24]{0:T(128)S(1)}, u32[]{:S(2)}) copy-start(s32[24]{0:T(128)S(1)} %add.177) | copy-start | bytes 292
  44.0 9.3 %collective-permute-start.11 = (f32[128,256]{1,0:T(8,128)S(1)}, f32[128,256]{1,0:T(8,128)}, u32[]{:S(2)}, u32[]{:S(2)}) collective-permute-start(f32[128,256]{1,0:T(8,128)S(1)} %get-tuple-element.28), channel_id=1, source_target_pairs={{0,12},{1,13},{2,14},{3,15},{4,0},{5,1},{6,2},{7,3},{8,4},{9,5},{1... | collective-permute-start | bytes 393224 | tf_op jit(solution)/shard_map/ppermute | solution.py:27
  151.1 40.2 %copy-start.39 = (f32[128,1,256]{2,0,1:T(8,128)}, f32[128,1,256]{2,0,1:T(8,128)S(1)}, u32[]{:S(2)}) copy-start(f32[128,1,256]{2,0,1:T(8,128)S(1)} %copy.243) | copy-start | bytes 393220
  151.1 11.0 %collective-permute-start.12 = (f32[1,128,256]{2,1,0:T(8,128)S(1)}, f32[1,128,256]{2,1,0:T(8,128)S(1)}, u32[]{:S(2)}, u32[]{:S(2)}) collective-permute-start(f32[1,128,256]{2,1,0:T(8,128)S(1)} %bitcast.569), channel_id=1, source_target_pairs={{0,16},{16,0},{1,17},{17,1},{2,18},{18,2},{3,19},{19,3},{4,20},{20... | collective-permute-start | bytes 393224 | tf_op jit(solution)/shard_map/ppermute | solution.py:16
  152.3 30.9 %copy-start.44 = (f32[128,1,256]{2,0,1:T(8,128)}, f32[128,1,256]{2,0,1:T(8,128)S(1)}, u32[]{:S(2)}) copy-start(f32[128,1,256]{2,0,1:T(8,128)S(1)} %copy.242) | copy-start | bytes 393220
  152.3 17.9 %collective-permute-start.13 = (f32[1,128,256]{2,1,0:T(8,128)S(1)}, f32[1,128,256]{2,1,0:T(8,128)}, u32[]{:S(2)}, u32[]{:S(2)}) collective-permute-start(f32[1,128,256]{2,1,0:T(8,128)S(1)} %bitcast.570), channel_id=1, source_target_pairs={{16,0},{0,16},{17,1},{1,17},{18,2},{2,18},{19,3},{3,19},{20,4},{4,... | collective-permute-start | bytes 393224 | tf_op jit(solution)/shard_map/ppermute | solution.py:19
  155.3 40.4 %copy-start.37 = (f32[128,1,256]{2,0,1:T(8,128)}, f32[128,1,256]{2,0,1:T(8,128)S(1)}, u32[]{:S(2)}) copy-start(f32[128,1,256]{2,0,1:T(8,128)S(1)} %copy.245) | copy-start | bytes 393220
  155.3 30.3 %copy-start.71 = (pred[256]{0:T(512)(128)(4,1)S(1)}, pred[256]{0:T(512)(128)(4,1)}, u32[]{:S(2)}) copy-start(pred[256]{0:T(512)(128)(4,1)} %copy-done.70) | copy-start | bytes 772
  155.3 18.9 %collective-permute-start.14 = (f32[1,128,256]{2,1,0:T(8,128)S(1)}, f32[1,128,256]{2,1,0:T(8,128)}, u32[]{:S(2)}, u32[]{:S(2)}) collective-permute-start(f32[1,128,256]{2,1,0:T(8,128)S(1)} %bitcast.567), channel_id=1, source_target_pairs={{0,1},{1,2},{2,3},{3,4},{4,5},{5,6},{6,7},{7,8},{8,9},{9,10},{10,1... | collective-permute-start | bytes 393224 | tf_op jit(solution)/shard_map/ppermute | solution.py:16
  155.5 38.0 %copy-start.38 = (f32[128,1,256]{2,0,1:T(8,128)}, f32[128,1,256]{2,0,1:T(8,128)S(1)}, u32[]{:S(2)}) copy-start(f32[128,1,256]{2,0,1:T(8,128)S(1)} %copy.244) | copy-start | bytes 393220
  155.5 22.7 %collective-permute-start.15 = (f32[1,128,256]{2,1,0:T(8,128)S(1)}, f32[1,128,256]{2,1,0:T(8,128)}, u32[]{:S(2)}, u32[]{:S(2)}) collective-permute-start(f32[1,128,256]{2,1,0:T(8,128)S(1)} %bitcast.568), channel_id=1, source_target_pairs={{1,0},{2,1},{3,2},{4,3},{5,4},{6,5},{7,6},{8,7},{9,8},{10,9},{11,1... | collective-permute-start | bytes 393224 | tf_op jit(solution)/shard_map/ppermute | solution.py:19
  161.0 38.2 %copy-start.31 = (f32[128,1,256]{2,0,1:T(8,128)}, f32[128,1,256]{2,0,1:T(8,128)S(1)}, u32[]{:S(2)}) copy-start(f32[128,1,256]{2,0,1:T(8,128)S(1)} %copy.247) | copy-start | bytes 393220
  161.0 21.3 %collective-permute-start.16 = (f32[128,256]{1,0:T(8,128)S(1)}, f32[128,256]{1,0:T(8,128)}, u32[]{:S(2)}, u32[]{:S(2)}) collective-permute-start(f32[128,256]{1,0:T(8,128)S(1)} %bitcast.565), channel_id=1, source_target_pairs={{0,4},{1,5},{2,6},{3,7},{4,8},{5,9},{6,10},{7,11},{8,12},{9,13},{1... | collective-permute-start | bytes 393224 | tf_op jit(solution)/shard_map/ppermute | solution.py:27
  162.1 35.8 %copy-start.33 = (f32[128,1,256]{2,0,1:T(8,128)}, f32[128,1,256]{2,0,1:T(8,128)S(1)}, u32[]{:S(2)}) copy-start(f32[128,1,256]{2,0,1:T(8,128)S(1)} %copy.246) | copy-start | bytes 393220
  162.1 25.8 %collective-permute-start.17 = (f32[128,256]{1,0:T(8,128)S(1)}, f32[128,256]{1,0:T(8,128)}, u32[]{:S(2)}, u32[]{:S(2)}) collective-permute-start(f32[128,256]{1,0:T(8,128)S(1)} %bitcast.566), channel_id=1, source_target_pairs={{0,12},{1,13},{2,14},{3,15},{4,0},{5,1},{6,2},{7,3},{8,4},{9,5},{1... | collective-permute-start | bytes 393224 | tf_op jit(solution)/shard_map/ppermute | solution.py:27
  168.5 22.7 %copy-start.69 = (pred[256]{0:T(512)(128)(4,1)S(1)}, pred[256]{0:T(512)(128)(4,1)}, u32[]{:S(2)}) copy-start(pred[256]{0:T(512)(128)(4,1)} %copy-done.68) | copy-start | bytes 772
  170.2 23.3 %copy-start.67 = (pred[256]{0:T(512)(128)(4,1)S(1)}, pred[256]{0:T(512)(128)(4,1)}, u32[]{:S(2)}) copy-start(pred[256]{0:T(512)(128)(4,1)} %copy-done.66) | copy-start | bytes 772
  171.2 24.6 %copy-start.65 = (pred[256]{0:T(512)(128)(4,1)S(1)}, pred[256]{0:T(512)(128)(4,1)}, u32[]{:S(2)}) copy-start(pred[256]{0:T(512)(128)(4,1)} %copy-done.64) | copy-start | bytes 772
  171.2 26.7 %copy-start.63 = (pred[256]{0:T(512)(128)(4,1)S(1)}, pred[256]{0:T(512)(128)(4,1)}, u32[]{:S(2)}) copy-start(pred[256]{0:T(512)(128)(4,1)} %copy-done.62) | copy-start | bytes 772
  172.5 26.7 %copy-start.61 = (pred[256]{0:T(512)(128)(4,1)S(1)}, pred[256]{0:T(512)(128)(4,1)}, u32[]{:S(2)}) copy-start(pred[256]{0:T(512)(128)(4,1)} %copy-done.60) | copy-start | bytes 772
  205.7 6.5 %collective-permute-start.18 = (f32[1,128,256]{2,1,0:T(8,128)S(1)}, f32[1,128,256]{2,1,0:T(8,128)S(1)}, u32[]{:S(2)}, u32[]{:S(2)}) collective-permute-start(f32[1,128,256]{2,1,0:T(8,128)S(1)} %get-tuple-element.21), channel_id=1, source_target_pairs={{0,16},{16,0},{1,17},{17,1},{2,18},{18,2},{3,19},{19,3},{4,20},{20... | collective-permute-start | bytes 393224 | tf_op jit(solution)/shard_map/ppermute | solution.py:16
  205.8 14.2 %collective-permute-start.19 = (f32[1,128,256]{2,1,0:T(8,128)}, f32[1,128,256]{2,1,0:T(8,128)}, u32[]{:S(2)}, u32[]{:S(2)}) collective-permute-start(f32[1,128,256]{2,1,0:T(8,128)} %get-tuple-element.17), channel_id=1, source_target_pairs={{16,0},{0,16},{17,1},{1,17},{18,2},{2,18},{19,3},{3,19},{20,4},{4,... | collective-permute-start | bytes 393224 | tf_op jit(solution)/shard_map/ppermute | solution.py:19
  207.7 16.3 %collective-permute-start.20 = (f32[1,128,256]{2,1,0:T(8,128)}, f32[1,128,256]{2,1,0:T(8,128)}, u32[]{:S(2)}, u32[]{:S(2)}) collective-permute-start(f32[1,128,256]{2,1,0:T(8,128)} %get-tuple-element.20), channel_id=1, source_target_pairs={{0,1},{1,2},{2,3},{3,4},{4,5},{5,6},{6,7},{7,8},{8,9},{9,10},{10,1... | collective-permute-start | bytes 393224 | tf_op jit(solution)/shard_map/ppermute | solution.py:16
  207.7 20.3 %collective-permute-start.21 = (f32[1,128,256]{2,1,0:T(8,128)}, f32[1,128,256]{2,1,0:T(8,128)}, u32[]{:S(2)}, u32[]{:S(2)}) collective-permute-start(f32[1,128,256]{2,1,0:T(8,128)} %get-tuple-element.18), channel_id=1, source_target_pairs={{1,0},{2,1},{3,2},{4,3},{5,4},{6,5},{7,6},{8,7},{9,8},{10,9},{11,1... | collective-permute-start | bytes 393224 | tf_op jit(solution)/shard_map/ppermute | solution.py:19
  212.2 19.9 %collective-permute-start.22 = (f32[128,256]{1,0:T(8,128)}, f32[128,256]{1,0:T(8,128)}, u32[]{:S(2)}, u32[]{:S(2)}) collective-permute-start(f32[128,256]{1,0:T(8,128)} %get-tuple-element.19), channel_id=1, source_target_pairs={{0,4},{1,5},{2,6},{3,7},{4,8},{5,9},{6,10},{7,11},{8,12},{9,13},{1... | collective-permute-start | bytes 393224 | tf_op jit(solution)/shard_map/ppermute | solution.py:27
  212.2 26.1 %collective-permute-start.23 = (f32[128,256]{1,0:T(8,128)}, f32[128,256]{1,0:T(8,128)}, u32[]{:S(2)}, u32[]{:S(2)}) collective-permute-start(f32[128,256]{1,0:T(8,128)} %get-tuple-element.16), channel_id=1, source_target_pairs={{0,12},{1,13},{2,14},{3,15},{4,0},{5,1},{6,2},{7,3},{8,4},{9,5},{1... | collective-permute-start | bytes 393224 | tf_op jit(solution)/shard_map/ppermute | solution.py:27
  241.6 50.7 %copy-start.46 = (f32[256,128]{0,1:T(8,128)}, f32[256,128]{0,1:T(8,128)S(1)}, u32[]{:S(2)}) copy-start(f32[256,128]{0,1:T(8,128)S(1)} %copy.216) | copy-start | bytes 393220
  253.5 85.2 %copy-start.72 = (f32[3,96]{1,0:T(4,128)S(1)}, f32[3,96]{1,0:T(4,128)}, u32[]{:S(2)}) copy-start(f32[3,96]{1,0:T(4,128)} %param.14) | copy-start | bytes 3460
  296.7 103.6 %copy-start.14 = (f32[128,1,256]{2,0,1:T(8,128)S(1)}, f32[128,1,256]{2,0,1:T(8,128)}, u32[]{:S(2)}) copy-start(f32[128,1,256]{2,0,1:T(8,128)} %copy-done.13) | copy-start | bytes 393220
  338.8 56.0 %copy-start.79 = (f32[128]{0:T(128)S(1)}, f32[128]{0:T(128)}, u32[]{:S(2)}) copy-start(f32[128]{0:T(128)} %get-tuple-element.5) | copy-start | bytes 1540
  381.3 18.9 %copy-start.24 = (f32[256,128]{0,1:T(8,128)S(1)}, f32[256,128]{0,1:T(8,128)}, u32[]{:S(2)}) copy-start(f32[256,128]{0,1:T(8,128)} %copy-done.23) | copy-start | bytes 393220
  381.3 18.9 %copy-start.36 = (f32[256,128]{0,1:T(8,128)S(1)}, f32[256,128]{0,1:T(8,128)}, u32[]{:S(2)}) copy-start(f32[256,128]{0,1:T(8,128)} %copy-done.35) | copy-start | bytes 393220
  381.3 18.9 %copy-start.45 = (f32[128,1,256]{2,0,1:T(8,128)S(1)}, f32[128,1,256]{2,0,1:T(8,128)}, u32[]{:S(2)}) copy-start(f32[128,1,256]{2,0,1:T(8,128)} %copy-done.44) | copy-start | bytes 393220
  381.4 18.9 %copy-start.48 = (f32[256,128]{0,1:T(8,128)S(1)}, f32[256,128]{0,1:T(8,128)}, u32[]{:S(2)}) copy-start(f32[256,128]{0,1:T(8,128)} %copy.190) | copy-start | bytes 393220
  383.2 12.3 %collective-permute-start.24 = (f32[1,128,256]{2,1,0:T(8,128)S(1)}, f32[1,128,256]{2,1,0:T(8,128)S(1)}, u32[]{:S(2)}, u32[]{:S(2)}) collective-permute-start(f32[1,128,256]{2,1,0:T(8,128)S(1)} %bitcast.574), channel_id=1, source_target_pairs={{0,16},{16,0},{1,17},{17,1},{2,18},{18,2},{3,19},{19,3},{4,20},{20... | collective-permute-start | bytes 393224 | tf_op jit(solution)/shard_map/ppermute | solution.py:16
  384.5 17.3 %collective-permute-start.25 = (f32[1,128,256]{2,1,0:T(8,128)S(1)}, f32[1,128,256]{2,1,0:T(8,128)}, u32[]{:S(2)}, u32[]{:S(2)}) collective-permute-start(f32[1,128,256]{2,1,0:T(8,128)S(1)} %bitcast.575), channel_id=1, source_target_pairs={{16,0},{0,16},{17,1},{1,17},{18,2},{2,18},{19,3},{3,19},{20,4},{4,... | collective-permute-start | bytes 393224 | tf_op jit(solution)/shard_map/ppermute | solution.py:19
  387.4 17.0 %collective-permute-start.26 = (f32[1,128,256]{2,1,0:T(8,128)S(1)}, f32[1,128,256]{2,1,0:T(8,128)}, u32[]{:S(2)}, u32[]{:S(2)}) collective-permute-start(f32[1,128,256]{2,1,0:T(8,128)S(1)} %bitcast.572), channel_id=1, source_target_pairs={{0,1},{1,2},{2,3},{3,4},{4,5},{5,6},{6,7},{7,8},{8,9},{9,10},{10,1... | collective-permute-start | bytes 393224 | tf_op jit(solution)/shard_map/ppermute | solution.py:16
  388.5 20.2 %copy-start.54 = (f32[128,1,256]{2,0,1:T(8,128)}, f32[128,1,256]{2,0,1:T(8,128)S(1)}, u32[]{:S(2)}) copy-start(f32[128,1,256]{2,0,1:T(8,128)S(1)} %copy.250) | copy-start | bytes 393220
  388.5 18.4 %collective-permute-start.27 = (f32[1,128,256]{2,1,0:T(8,128)S(1)}, f32[1,128,256]{2,1,0:T(8,128)}, u32[]{:S(2)}, u32[]{:S(2)}) collective-permute-start(f32[1,128,256]{2,1,0:T(8,128)S(1)} %bitcast.573), channel_id=1, source_target_pairs={{1,0},{2,1},{3,2},{4,3},{5,4},{6,5},{7,6},{8,7},{9,8},{10,9},{11,1... | collective-permute-start | bytes 393224 | tf_op jit(solution)/shard_map/ppermute | solution.py:19
  394.0 15.5 %collective-permute-start.28 = (f32[128,256]{1,0:T(8,128)S(1)}, f32[128,256]{1,0:T(8,128)}, u32[]{:S(2)}, u32[]{:S(2)}) collective-permute-start(f32[128,256]{1,0:T(8,128)S(1)} %bitcast.571), channel_id=1, source_target_pairs={{0,4},{1,5},{2,6},{3,7},{4,8},{5,9},{6,10},{7,11},{8,12},{9,13},{1... | collective-permute-start | bytes 393224 | tf_op jit(solution)/shard_map/ppermute | solution.py:27
  395.5 16.5 %collective-permute-start.29 = (f32[128,256]{1,0:T(8,128)}, f32[128,256]{1,0:T(8,128)}, u32[]{:S(2)}, u32[]{:S(2)}) collective-permute-start(f32[128,256]{1,0:T(8,128)} %bitcast.155), channel_id=1, source_target_pairs={{0,12},{1,13},{2,14},{3,15},{4,0},{5,1},{6,2},{7,3},{8,4},{9,5},{1... | collective-permute-start | bytes 393224 | tf_op jit(solution)/shard_map/ppermute | solution.py:27
  (47 other events, 534.1 us)
where the time goes:
time: 434 us; the launch traced here: 432 us
  blocking collectives  199 us (46%)
  local copies, waits for them, and re-layouts  101 us (23%)
  starting transfers between devices  53.7 us (12%)
  other arithmetic  53 us (12%)
  matrix products  23.3 us (5%)
    all_gather x2, blocking collectives, local(): lax.all_gather(own_values, ('cluster', 'sub'), axis=1, tiled=True)  82.9 us
    psum x2, blocking collectives, local(): lax.psum((coarse_local, local_curve), ('cluster', 'sub'))  79.2 us
    gather x60, local copies, waits for them, and re-layouts, assemble(): permuted = jnp.take(received[face_index], slot_maps[face_index], axis=1)  55.5 us
    unnamed x25, other arithmetic  39.7 us
    psum x1, blocking collectives, precond_with_product(): lax.psum(jnp.sum(vector * precond, axis=1), ('cluster', 'sub'))  36.9 us
    ppermute x10, starting transfers between devices, padded(): lax.ppermute(lax.slice_in_dim(block, 0, width, axis=dim), axis, backward)  28.2 us
    unnamed x184, local copies, waits for them, and re-layouts  20.4 us
    ppermute x10, starting transfers between devices, passed_along(): return lax.ppermute(value, axis, pairs)  19.6 us
  transfers between devices with their start and end apart: 30, of which 0 were waited for; matrix products, arithmetic and copies ran while one was open for 20% of the time, Pallas kernels for 0%

commit v1 on v0

--- a/solution.py
+++ b/solution.py
@@ -5,6 +5,18 @@
 
 ITERS = 2
 STRIDE = 4
+
+
+def gather_by_bits(x, axis, dim):
+    ways, here = (lax.axis_size(axis), lax.axis_index(axis))
+    grown, reach = (x, 1)
+    while reach < ways:
+        theirs = lax.ppermute(grown, axis, [(d, d ^ reach) for d in range(ways)])
+        mine_first = jnp.concatenate([grown, theirs], axis=dim)
+        theirs_first = jnp.concatenate([theirs, grown], axis=dim)
+        grown = jnp.where(here & reach == 0, mine_first, theirs_first)
+        reach = 2 * reach
+    return grown
 
 
 def padded(block, sides, width):
@@ -95,7 +107,7 @@
         local_curve = jnp.sum(direction * direct, axis=1)
         apply_coarse_load, curve_total = lax.psum((coarse_local, local_curve), ("cluster", "sub"))
         own_values = jnp.dot(apply_coarse_load, coarse_inverse.T, precision=lax.Precision.HIGHEST)
-        solution = lax.all_gather(own_values, ("cluster", "sub"), axis=1, tiled=True)
+        solution = gather_by_bits(own_values, ("cluster", "sub"), 1)
         corner_values = jnp.dot(solution, spread.T, precision=lax.Precision.HIGHEST).astype(
             jnp.bfloat16
         )

time: 434 us -> 390 us (0.90)
  blocking collectives: 199 us -> 118 us
  waiting for transfers between devices: 0.08 us -> 21.3 us
  starting transfers between devices: 53.7 us -> 67.9 us
    all_gather x2 -> x0, blocking collectives: 82.9 us -> none  [local(): lax.all_gather(own_values, ('cluster', 'sub'), axis=1, tiled=True)]
    ppermute x0 -> x10, waiting for transfers between devices: none -> 21.3 us  [gather_by_bits(): theirs = lax.ppermute(grown, axis, [(d, d ^ reach) for d in range(ways)])]
    ppermute x0 -> x10, starting transfers between devices: none -> 14.1 us  [gather_by_bits(): theirs = lax.ppermute(grown, axis, [(d, d ^ reach) for d in range(ways)])]
    ppermute x10, starting transfers between devices: 28.2 us -> 22.6 us  [padded(): lax.ppermute(lax.slice_in_dim(block, 0, width, axis=dim), axis, backward)]
    ppermute x10, starting transfers between devices: 5.88 us -> 11.4 us  [padded(): lax.ppermute(lax.slice_in_dim(block, block.shape[dim] - width, None, axis...]
    unnamed x184 -> x212, local copies, waits for them, and re-layouts: 20.4 us -> 19.9 us
  transfers between devices with their start and end apart: 30 -> 40, of which waited for: 0 -> 10; matrix products, arithmetic and copies ran while one was open for 20% -> 23% of each run, Pallas kernels for 0% -> 0%
where the time goes in v1:
time: 390 us; the launch traced here: 388 us
  blocking collectives  118 us (30%)
  local copies, waits for them, and re-layouts  101 us (26%)
  starting transfers between devices  67.9 us (17%)
  other arithmetic  54 us (14%)
  matrix products  22.2 us (6%)
  waiting for transfers between devices  21.3 us (5%)
    psum x2, blocking collectives, local(): lax.psum((coarse_local, local_curve), ('cluster', 'sub'))  81 us
    gather x60, local copies, waits for them, and re-layouts, assemble(): permuted = jnp.take(received[face_index], slot_maps[face_index], axis=1)  54.7 us
    unnamed x25, other arithmetic  39.6 us
    psum x1, blocking collectives, precond_with_product(): lax.psum(jnp.sum(vector * precond, axis=1), ('cluster', 'sub'))  36.9 us
    ppermute x10, starting transfers between devices, padded(): lax.ppermute(lax.slice_in_dim(block, 0, width, axis=dim), axis, backward)  22.6 us
    ppermute x10, waiting for transfers between devices, gather_by_bits(): theirs = lax.ppermute(grown, axis, [(d, d ^ reach) for d in range(ways)])  21.3 us
    unnamed x212, local copies, waits for them, and re-layouts  19.9 us
    ppermute x10, starting transfers between devices, passed_along(): return lax.ppermute(value, axis, pairs)  19.8 us
  transfers between devices with their start and end apart: 40, of which 10 were waited for; matrix products, arithmetic and copies ran while one was open for 23% of the time, Pallas kernels for 0%

profile of v1, /device:TPU:0, one launch (start us, length us, event | category | flops | bytes accessed | tf_op | source)
XLA Modules:
  0.0 387.6 jit_solution(3260936831795916987)
XLA Ops:
  2.3 3.0 collective-permute-start
  5.8 4.5 %collective-permute-start.3 = (f32[1,128,256]{2,1,0:T(8,128)S(1)}, f32[1,128,256]{2,1,0:T(8,128)S(1)}, u32[]{:S(2)}, u32[]{:S(2)}) collective-permute-start(f32[1,128,256]{2,1,0:T(8,128)S(1)} %bitcast.543), channel_id=1, source_target_pairs={{1,0},{2,1},{3,2},{4,3},{5,4},{6,5},{7,6},{8,7},{9,8},{10,9},{11,1... | collective-permute-start | bytes 393224 | tf_op jit(solution)/shard_map/ppermute | solution.py:31
  12.6 3.6 collective-permute-start.5
  16.2 6.6 %copy.91 = bf16[1,1536,1536]{1,2,0:T(8,128)(2,1)} copy(bf16[1,1536,1536]{2,1,0:T(8,128)(2,1)} %param.12) | data formatting | bytes 9437184 | tf_op args[2]
  33.0 4.0 %fusion.6 = f32[128,6,256]{2,0,1:T(8,128)S(1)} fusion(bf16[6,256,1536]{2,1,0:T(8,128)(2,1)} %bitcast.536, f32[128,1536]{1,0:T(8,128)S(1)} %constant_dynamic-update-slice_fusion), kind=kOutput, calls=%fused_computation.48 | convolution fusion | flops 604176384 | bytes 6291456 | tf_op jit(solution)/shard_map/dot_general | solution.py:90
  37.7 2.0 collective-permute-start.6
  39.7 4.4 %collective-permute-start.9 = (f32[1,128,256]{2,1,0:T(8,128)S(1)}, f32[1,128,256]{2,1,0:T(8,128)S(1)}, u32[]{:S(2)}, u32[]{:S(2)}) collective-permute-start(f32[1,128,256]{2,1,0:T(8,128)S(1)} %get-tuple-element.30), channel_id=1, source_target_pairs={{1,0},{2,1},{3,2},{4,3},{5,4},{6,5},{7,6},{8,7},{9,8},{10,9},{11,1... | collective-permute-start | bytes 393224 | tf_op jit(solution)/shard_map/ppermute | solution.py:31
  44.9 3.8 collective-permute-start.11
  59.1 3.8 multiply_reduce_fusion.3
  63.5 37.7 %all-reduce.1 = (f32[128,96]{0,1:T(8,128)S(1)}, f32[128]{0:T(128)}, f32[128]{0:T(128)}) all-reduce(f32[128,96]{0,1:T(8,128)S(1)} %fusion.53, f32[128]{0:T(128)} %get-tuple-element.4, f32[128]{0:T(128)} %get-tuple-element.3), channel_id=1, replica_groups=mesh['cluster'=2,'sub'=16] {'cluster','sub'}, use_global_device_ids=true, to_apply=%region_4.6 | all-reduce | flops 12544 | bytes 100352 | tf_op jit(solution)/shard_map/psum | solution.py:108
  103.2 2.3 collective-permute-start.13
  105.6 1.6 collective-permute-done.13
  107.1 2.8 collective-permute-start.14
  110.0 1.6 collective-permute-done.14
  111.6 2.3 collective-permute-start.15
  114.0 2.3 collective-permute-done.15
  116.3 2.0 collective-permute-start.16
  118.3 1.8 collective-permute-done.16
  125.4 2.1 collective-permute-start.17
  129.8 4.5 %collective-permute-start.20 = (f32[1,128,256]{2,1,0:T(8,128)S(1)}, f32[1,128,256]{2,1,0:T(8,128)}, u32[]{:S(2)}, u32[]{:S(2)}) collective-permute-start(f32[1,128,256]{2,1,0:T(8,128)S(1)} %bitcast.550), channel_id=1, source_target_pairs={{1,0},{2,1},{3,2},{4,3},{5,4},{6,5},{7,6},{8,7},{9,8},{10,9},{11,1... | collective-permute-start | bytes 393224 | tf_op jit(solution)/shard_map/ppermute | solution.py:31
  138.1 3.8 collective-permute-start.22
  144.3 1.6 copy.108
  148.3 1.7 copy.110
  152.3 1.7 copy.114
  156.3 1.7 copy.116
  161.4 2.2 constant_dynamic-update-slice_fusion.17
  167.0 2.2 constant_dynamic-update-slice_fusion.16
  169.1 2.1 constant_dynamic-update-slice_fusion.15
  171.3 2.2 constant_dynamic-update-slice_fusion.14
  176.0 4.3 %fusion.4 = f32[128,6,256]{2,0,1:T(8,128)S(1)} fusion(bf16[6,256,1536]{2,1,0:T(8,128)(2,1)} %bitcast.537, f32[128,1536]{1,0:T(8,128)S(1)} %constant_dynamic-update-slice_fusion, f32[128,1536]{1,0:T(8,128)} %constant_dynamic-update-slice_fusion.12, f32[128]{0:T(128)S(1)} %add_divide_fusion.1), kind=kOutput, calls=%fused_computation.46 | convolution fusion | flops 604569600 | bytes 7078400 | tf_op jit(solution)/shard_map/dot_general | solution.py:90
  181.1 2.0 collective-permute-start.23
  183.2 4.4 %collective-permute-start.26 = (f32[1,128,256]{2,1,0:T(8,128)}, f32[1,128,256]{2,1,0:T(8,128)}, u32[]{:S(2)}, u32[]{:S(2)}) collective-permute-start(f32[1,128,256]{2,1,0:T(8,128)} %get-tuple-element.18), channel_id=1, source_target_pairs={{1,0},{2,1},{3,2},{4,3},{5,4},{6,5},{7,6},{8,7},{9,8},{10,9},{11,1... | collective-permute-start | bytes 393224 | tf_op jit(solution)/shard_map/ppermute | solution.py:31
  187.6 3.8 collective-permute-start.28
  193.8 1.7 copy.124
  197.8 1.7 copy.126
  201.8 1.7 copy.128
  205.8 1.7 copy.130
  209.9 1.7 copy.132
  211.5 2.2 constant_dynamic-update-slice_fusion.23
  217.0 2.2 constant_dynamic-update-slice_fusion.22
  219.2 2.1 constant_dynamic-update-slice_fusion.21
  221.4 2.2 constant_dynamic-update-slice_fusion.20
  223.6 2.2 constant_dynamic-update-slice_fusion.19
  227.0 1.7 multiply_reduce_fusion.1
  228.7 36.9 %psum.45 = f32[128]{0:T(128)S(1)} all-reduce(f32[128]{0:T(128)S(1)} %multiply_reduce_fusion.1), channel_id=1, replica_groups=mesh['cluster'=2,'sub'=16] {'cluster','sub'}, use_global_device_ids=true, to_apply=%region_7.9 | all-reduce | flops 128 | bytes 1024 | tf_op jit(solution)/shard_map/psum | solution.py:94
  267.1 3.8 multiply_reduce_fusion
  271.2 43.3 %all-reduce = (f32[128]{0:T(128)}, f32[128,96]{0,1:T(8,128)S(1)}) all-reduce(f32[128]{0:T(128)S(1)} %get-tuple-element.85, f32[128,96]{0,1:T(8,128)S(1)} %fusion.52), channel_id=1, replica_groups=mesh['cluster'=2,'sub'=16] {'cluster','sub'}, use_global_device_ids=true, to_apply=%region_9.11 | all-reduce | flops 12416 | bytes 99328 | tf_op jit(solution)/shard_map/psum | solution.py:108
  315.9 2.3 collective-permute-start.30
  318.2 1.6 collective-permute-done.30
  319.9 3.6 collective-permute-done.31
  323.7 4.5 %collective-permute-done.32 = f32[128,24]{0,1:T(8,128)S(1)} collective-permute-done((f32[128,24]{0,1:T(8,128)S(1)}, f32[128,24]{0,1:T(8,128)S(1)}, u32[]{:S(2)}, u32[]{:S(2)}) %collective-permute-start.32) | collective-permute-done | bytes 12320 | tf_op jit(solution)/shard_map/ppermute | solution.py:14
  328.2 2.0 collective-permute-start.33
  330.2 1.8 collective-permute-done.33
  335.4 2.1 collective-permute-start.34
  340.6 4.5 %collective-permute-start.37 = (f32[1,128,256]{2,1,0:T(8,128)S(1)}, f32[1,128,256]{2,1,0:T(8,128)}, u32[]{:S(2)}, u32[]{:S(2)}) collective-permute-start(f32[1,128,256]{2,1,0:T(8,128)S(1)} %bitcast.555), channel_id=1, source_target_pairs={{1,0},{2,1},{3,2},{4,3},{5,4},{6,5},{7,6},{8,7},{9,8},{10,9},{11,1... | collective-permute-start | bytes 393224 | tf_op jit(solution)/shard_map/ppermute | solution.py:31
  348.4 4.1 %collective-permute-start.39 = (f32[128,256]{1,0:T(8,128)}, f32[128,256]{1,0:T(8,128)}, u32[]{:S(2)}, u32[]{:S(2)}) collective-permute-start(f32[128,256]{1,0:T(8,128)} %bitcast.149), channel_id=1, source_target_pairs={{0,12},{1,13},{2,14},{3,15},{4,0},{5,1},{6,2},{7,3},{8,4},{9,5},{1... | collective-permute-start | bytes 393224 | tf_op jit(solution)/shard_map/ppermute | solution.py:39
  354.5 2.1 bitcast_dynamic-update-slice_fusion.11
  368.4 1.6 gather_fusion.29
  370.0 1.7 copy.153
  371.8 2.8 bitcast_dynamic-update-slice_fusion.10
  374.6 2.6 bitcast_dynamic-update-slice_fusion.9
  377.2 2.7 bitcast_dynamic-update-slice_fusion.8
  380.0 2.4 bitcast_dynamic-update-slice_fusion.7
  383.9 3.8 multiply_subtract_fusion
  (411 shorter events, 103.3 us)
Async XLA Ops:
  0.6 62.3 %copy-start = (bf16[1,1536,24]{1,2,0:T(8,128)(2,1)S(1)}, bf16[1,1536,24]{1,2,0:T(8,128)(2,1)}, u32[]{:S(2)}) copy-start(bf16[1,1536,24]{1,2,0:T(8,128)(2,1)} %param.13) | copy-start | bytes 221188
  2.3 10.3 %collective-permute-start = (f32[1,128,256]{2,1,0:T(8,128)S(1)}, f32[1,128,256]{2,1,0:T(8,128)S(1)}, u32[]{:S(2)}, u32[]{:S(2)}) collective-permute-start(f32[1,128,256]{2,1,0:T(8,128)S(1)} %bitcast.545), channel_id=1, source_target_pairs={{0,16},{16,0},{1,17},{17,1},{2,18},{18,2},{3,19},{19,3},{4,20},{20... | collective-permute-start | bytes 393224 | tf_op jit(solution)/shard_map/ppermute | solution.py:28
  5.4 19.0 %collective-permute-start.1 = (f32[1,128,256]{2,1,0:T(8,128)S(1)}, f32[1,128,256]{2,1,0:T(8,128)S(1)}, u32[]{:S(2)}, u32[]{:S(2)}) collective-permute-start(f32[1,128,256]{2,1,0:T(8,128)S(1)} %bitcast.546), channel_id=1, source_target_pairs={{16,0},{0,16},{17,1},{1,17},{18,2},{2,18},{19,3},{3,19},{20,4},{4,... | collective-permute-start | bytes 393224 | tf_op jit(solution)/shard_map/ppermute | solution.py:31
  5.6 19.7 %collective-permute-start.2 = (f32[1,128,256]{2,1,0:T(8,128)S(1)}, f32[1,128,256]{2,1,0:T(8,128)S(1)}, u32[]{:S(2)}, u32[]{:S(2)}) collective-permute-start(f32[1,128,256]{2,1,0:T(8,128)S(1)} %bitcast.542), channel_id=1, source_target_pairs={{0,1},{1,2},{2,3},{3,4},{4,5},{5,6},{6,7},{7,8},{8,9},{9,10},{10,1... | collective-permute-start | bytes 393224 | tf_op jit(solution)/shard_map/ppermute | solution.py:28
  5.8 20.5 %collective-permute-start.3 = (f32[1,128,256]{2,1,0:T(8,128)S(1)}, f32[1,128,256]{2,1,0:T(8,128)S(1)}, u32[]{:S(2)}, u32[]{:S(2)}) collective-permute-start(f32[1,128,256]{2,1,0:T(8,128)S(1)} %bitcast.543), channel_id=1, source_target_pairs={{1,0},{2,1},{3,2},{4,3},{5,4},{6,5},{7,6},{8,7},{9,8},{10,9},{11,1... | collective-permute-start | bytes 393224 | tf_op jit(solution)/shard_map/ppermute | solution.py:31
  10.4 16.9 %collective-permute-start.4 = (f32[128,256]{1,0:T(8,128)S(1)}, f32[128,256]{1,0:T(8,128)S(1)}, u32[]{:S(2)}, u32[]{:S(2)}) collective-permute-start(f32[128,256]{1,0:T(8,128)S(1)} %bitcast.541), channel_id=1, source_target_pairs={{0,4},{1,5},{2,6},{3,7},{4,8},{5,9},{6,10},{7,11},{8,12},{9,13},{1... | collective-permute-start | bytes 393224 | tf_op jit(solution)/shard_map/ppermute | solution.py:39
  11.5 42.0 %copy-start.84 = (pred[256]{0:T(512)(128)(4,1)}, pred[256]{0:T(512)(128)(4,1)S(1)}, u32[]{:S(2)}) copy-start(pred[256]{0:T(512)(128)(4,1)S(1)} %compare_and_fusion.5) | copy-start | bytes 772
  11.5 44.4 %copy-start.81 = (pred[256]{0:T(512)(128)(4,1)}, pred[256]{0:T(512)(128)(4,1)S(1)}, u32[]{:S(2)}) copy-start(pred[256]{0:T(512)(128)(4,1)S(1)} %compare_and_fusion.4) | copy-start | bytes 772
  11.6 45.0 %copy-start.78 = (pred[256]{0:T(512)(128)(4,1)}, pred[256]{0:T(512)(128)(4,1)S(1)}, u32[]{:S(2)}) copy-start(pred[256]{0:T(512)(128)(4,1)S(1)} %compare_and_fusion.3) | copy-start | bytes 772
  11.6 45.6 %copy-start.75 = (pred[256]{0:T(512)(128)(4,1)}, pred[256]{0:T(512)(128)(4,1)S(1)}, u32[]{:S(2)}) copy-start(pred[256]{0:T(512)(128)(4,1)S(1)} %compare_and_fusion.2) | copy-start | bytes 772
  11.6 46.2 %copy-start.72 = (pred[256]{0:T(512)(128)(4,1)}, pred[256]{0:T(512)(128)(4,1)S(1)}, u32[]{:S(2)}) copy-start(pred[256]{0:T(512)(128)(4,1)S(1)} %compare_and_fusion.1) | copy-start | bytes 772
  11.7 46.8 %copy-start.69 = (pred[256]{0:T(512)(128)(4,1)}, pred[256]{0:T(512)(128)(4,1)S(1)}, u32[]{:S(2)}) copy-start(pred[256]{0:T(512)(128)(4,1)S(1)} %compare_and_fusion) | copy-start | bytes 772
  11.7 180.8 %copy-start.68 = (s32[1024]{0:T(1024)}, s32[1024]{0:T(1024)S(1)}, u32[]{:S(2)}) copy-start(s32[1024]{0:T(1024)S(1)} %pad_clamp_fusion.5) | copy-start | bytes 12292
  11.7 184.7 %copy-start.67 = (s32[1024]{0:T(1024)}, s32[1024]{0:T(1024)S(1)}, u32[]{:S(2)}) copy-start(s32[1024]{0:T(1024)S(1)} %pad_clamp_fusion.4) | copy-start | bytes 12292
  11.7 188.7 %copy-start.66 = (s32[1024]{0:T(1024)}, s32[1024]{0:T(1024)S(1)}, u32[]{:S(2)}) copy-start(s32[1024]{0:T(1024)S(1)} %pad_clamp_fusion.3) | copy-start | bytes 12292
  12.4 192.1 %copy-start.65 = (s32[1024]{0:T(1024)}, s32[1024]{0:T(1024)S(1)}, u32[]{:S(2)}) copy-start(s32[1024]{0:T(1024)S(1)} %pad_clamp_fusion.2) | copy-start | bytes 12292
  12.5 196.0 %copy-start.64 = (s32[1024]{0:T(1024)}, s32[1024]{0:T(1024)S(1)}, u32[]{:S(2)}) copy-start(s32[1024]{0:T(1024)S(1)} %pad_clamp_fusion.1) | copy-start | bytes 12292
  12.6 15.6 %collective-permute-start.5 = (f32[128,256]{1,0:T(8,128)S(1)}, f32[128,256]{1,0:T(8,128)S(1)}, u32[]{:S(2)}, u32[]{:S(2)}) collective-permute-start(f32[128,256]{1,0:T(8,128)S(1)} %bitcast.544), channel_id=1, source_target_pairs={{0,12},{1,13},{2,14},{3,15},{4,0},{5,1},{6,2},{7,3},{8,4},{9,5},{1... | collective-permute-start | bytes 393224 | tf_op jit(solution)/shard_map/ppermute | solution.py:39
  16.2 198.5 %copy-start.63 = (s32[1024]{0:T(1024)}, s32[1024]{0:T(1024)S(1)}, u32[]{:S(2)}) copy-start(s32[1024]{0:T(1024)S(1)} %pad_clamp_fusion) | copy-start | bytes 12292
  37.7 7.2 %collective-permute-start.6 = (f32[1,128,256]{2,1,0:T(8,128)S(1)}, f32[1,128,256]{2,1,0:T(8,128)S(1)}, u32[]{:S(2)}, u32[]{:S(2)}) collective-permute-start(f32[1,128,256]{2,1,0:T(8,128)S(1)} %get-tuple-element.33), channel_id=1, source_target_pairs={{0,16},{16,0},{1,17},{17,1},{2,18},{18,2},{3,19},{19,3},{4,20},{20... | collective-permute-start | bytes 393224 | tf_op jit(solution)/shard_map/ppermute | solution.py:28
  39.7 9.9 %collective-permute-start.7 = (f32[1,128,256]{2,1,0:T(8,128)S(1)}, f32[1,128,256]{2,1,0:T(8,128)S(1)}, u32[]{:S(2)}, u32[]{:S(2)}) collective-permute-start(f32[1,128,256]{2,1,0:T(8,128)S(1)} %get-tuple-element.29), channel_id=1, source_target_pairs={{16,0},{0,16},{17,1},{1,17},{18,2},{2,18},{19,3},{3,19},{20,4},{4,... | collective-permute-start | bytes 393224 | tf_op jit(solution)/shard_map/ppermute | solution.py:31
  39.7 10.9 %collective-permute-start.8 = (f32[1,128,256]{2,1,0:T(8,128)S(1)}, f32[1,128,256]{2,1,0:T(8,128)S(1)}, u32[]{:S(2)}, u32[]{:S(2)}) collective-permute-start(f32[1,128,256]{2,1,0:T(8,128)S(1)} %get-tuple-element.32), channel_id=1, source_target_pairs={{0,1},{1,2},{2,3},{3,4},{4,5},{5,6},{6,7},{7,8},{8,9},{9,10},{10,1... | collective-permute-start | bytes 393224 | tf_op jit(solution)/shard_map/ppermute | solution.py:28
  39.7 11.8 %collective-permute-start.9 = (f32[1,128,256]{2,1,0:T(8,128)S(1)}, f32[1,128,256]{2,1,0:T(8,128)S(1)}, u32[]{:S(2)}, u32[]{:S(2)}) collective-permute-start(f32[1,128,256]{2,1,0:T(8,128)S(1)} %get-tuple-element.30), channel_id=1, source_target_pairs={{1,0},{2,1},{3,2},{4,3},{5,4},{6,5},{7,6},{8,7},{9,8},{10,9},{11,1... | collective-permute-start | bytes 393224 | tf_op jit(solution)/shard_map/ppermute | solution.py:31
  44.2 8.3 %collective-permute-start.10 = (f32[128,256]{1,0:T(8,128)S(1)}, f32[128,256]{1,0:T(8,128)S(1)}, u32[]{:S(2)}, u32[]{:S(2)}) collective-permute-start(f32[128,256]{1,0:T(8,128)S(1)} %get-tuple-element.31), channel_id=1, source_target_pairs={{0,4},{1,5},{2,6},{3,7},{4,8},{5,9},{6,10},{7,11},{8,12},{9,13},{1... | collective-permute-start | bytes 393224 | tf_op jit(solution)/shard_map/ppermute | solution.py:39
  44.9 9.2 %collective-permute-start.11 = (f32[128,256]{1,0:T(8,128)}, f32[128,256]{1,0:T(8,128)}, u32[]{:S(2)}, u32[]{:S(2)}) collective-permute-start(f32[128,256]{1,0:T(8,128)} %get-tuple-element.28), channel_id=1, source_target_pairs={{0,12},{1,13},{2,14},{3,15},{4,0},{5,1},{6,2},{7,3},{8,4},{9,5},{1... | collective-permute-start | bytes 393224 | tf_op jit(solution)/shard_map/ppermute | solution.py:39
  102.0 1.2 collective-permute-start.12
  103.2 3.9 %collective-permute-start.13 = (f32[128,6]{0,1:T(8,128)S(1)}, f32[128,6]{0,1:T(8,128)S(1)}, u32[]{:S(2)}, u32[]{:S(2)}) collective-permute-start(f32[128,6]{0,1:T(8,128)S(1)} %maximum_select_fusion.10), channel_id=1, source_target_pairs={{0,2},{1,3},{2,0},{3,1},{4,6},{5,7},{6,4},{7,5},{8,10},{9,11},{10,... | collective-permute-start | bytes 9224 | tf_op jit(solution)/shard_map/ppermute | solution.py:14
  107.1 4.5 %collective-permute-start.14 = (f32[128,12]{0,1:T(8,128)S(1)}, f32[128,12]{0,1:T(8,128)S(1)}, u32[]{:S(2)}, u32[]{:S(2)}) collective-permute-start(f32[128,12]{0,1:T(8,128)S(1)} %maximum_select_fusion.8), channel_id=1, source_target_pairs={{0,4},{1,5},{2,6},{3,7},{4,0},{5,1},{6,2},{7,3},{8,12},{9,13},{10,... | collective-permute-start | bytes 18440 | tf_op jit(solution)/shard_map/ppermute | solution.py:14
  111.6 4.7 %collective-permute-start.15 = (f32[128,24]{0,1:T(8,128)S(1)}, f32[128,24]{0,1:T(8,128)S(1)}, u32[]{:S(2)}, u32[]{:S(2)}) collective-permute-start(f32[128,24]{0,1:T(8,128)S(1)} %maximum_select_fusion.6), channel_id=1, source_target_pairs={{0,8},{1,9},{2,10},{3,11},{4,12},{5,13},{6,14},{7,15},{8,0},{9,1},... | collective-permute-start | bytes 36872 | tf_op jit(solution)/shard_map/ppermute | solution.py:14
  116.3 3.8 collective-permute-start.16
  125.4 41.5 %copy-start.39 = (f32[128,1,256]{2,0,1:T(8,128)}, f32[128,1,256]{2,0,1:T(8,128)S(1)}, u32[]{:S(2)}) copy-start(f32[128,1,256]{2,0,1:T(8,128)S(1)} %copy.161) | copy-start | bytes 393220
  125.4 12.7 %collective-permute-start.17 = (f32[1,128,256]{2,1,0:T(8,128)S(1)}, f32[1,128,256]{2,1,0:T(8,128)S(1)}, u32[]{:S(2)}, u32[]{:S(2)}) collective-permute-start(f32[1,128,256]{2,1,0:T(8,128)S(1)} %bitcast.551), channel_id=1, source_target_pairs={{0,16},{16,0},{1,17},{17,1},{2,18},{18,2},{3,19},{19,3},{4,20},{20... | collective-permute-start | bytes 393224 | tf_op jit(solution)/shard_map/ppermute | solution.py:28
  128.5 17.4 %collective-permute-start.18 = (f32[1,128,256]{2,1,0:T(8,128)S(1)}, f32[1,128,256]{2,1,0:T(8,128)}, u32[]{:S(2)}, u32[]{:S(2)}) collective-permute-start(f32[1,128,256]{2,1,0:T(8,128)S(1)} %bitcast.552), channel_id=1, source_target_pairs={{16,0},{0,16},{17,1},{1,17},{18,2},{2,18},{19,3},{3,19},{20,4},{4,... | collective-permute-start | bytes 393224 | tf_op jit(solution)/shard_map/ppermute | solution.py:31
  129.6 41.7 %copy-start.37 = (f32[128,1,256]{2,0,1:T(8,128)}, f32[128,1,256]{2,0,1:T(8,128)S(1)}, u32[]{:S(2)}) copy-start(f32[128,1,256]{2,0,1:T(8,128)S(1)} %copy.163) | copy-start | bytes 393220
  129.6 20.4 %collective-permute-start.19 = (f32[1,128,256]{2,1,0:T(8,128)S(1)}, f32[1,128,256]{2,1,0:T(8,128)}, u32[]{:S(2)}, u32[]{:S(2)}) collective-permute-start(f32[1,128,256]{2,1,0:T(8,128)S(1)} %bitcast.549), channel_id=1, source_target_pairs={{0,1},{1,2},{2,3},{3,4},{4,5},{5,6},{6,7},{7,8},{8,9},{9,10},{10,1... | collective-permute-start | bytes 393224 | tf_op jit(solution)/shard_map/ppermute | solution.py:28
  129.8 39.4 %copy-start.38 = (f32[128,1,256]{2,0,1:T(8,128)}, f32[128,1,256]{2,0,1:T(8,128)S(1)}, u32[]{:S(2)}) copy-start(f32[128,1,256]{2,0,1:T(8,128)S(1)} %copy.162) | copy-start | bytes 393220
  129.8 24.2 %collective-permute-start.20 = (f32[1,128,256]{2,1,0:T(8,128)S(1)}, f32[1,128,256]{2,1,0:T(8,128)}, u32[]{:S(2)}, u32[]{:S(2)}) collective-permute-start(f32[1,128,256]{2,1,0:T(8,128)S(1)} %bitcast.550), channel_id=1, source_target_pairs={{1,0},{2,1},{3,2},{4,3},{5,4},{6,5},{7,6},{8,7},{9,8},{10,9},{11,1... | collective-permute-start | bytes 393224 | tf_op jit(solution)/shard_map/ppermute | solution.py:31
  135.3 39.5 %copy-start.33 = (f32[128,1,256]{2,0,1:T(8,128)}, f32[128,1,256]{2,0,1:T(8,128)S(1)}, u32[]{:S(2)}) copy-start(f32[128,1,256]{2,0,1:T(8,128)S(1)} %copy.165) | copy-start | bytes 393220
  135.3 22.7 %collective-permute-start.21 = (f32[128,256]{1,0:T(8,128)S(1)}, f32[128,256]{1,0:T(8,128)}, u32[]{:S(2)}, u32[]{:S(2)}) collective-permute-start(f32[128,256]{1,0:T(8,128)S(1)} %bitcast.547), channel_id=1, source_target_pairs={{0,4},{1,5},{2,6},{3,7},{4,8},{5,9},{6,10},{7,11},{8,12},{9,13},{1... | collective-permute-start | bytes 393224 | tf_op jit(solution)/shard_map/ppermute | solution.py:39
  136.5 37.0 %copy-start.35 = (f32[128,1,256]{2,0,1:T(8,128)}, f32[128,1,256]{2,0,1:T(8,128)S(1)}, u32[]{:S(2)}) copy-start(f32[128,1,256]{2,0,1:T(8,128)S(1)} %copy.164) | copy-start | bytes 393220
  138.1 88.9 %copy-start.87 = (f32[128]{0:T(128)}, f32[128]{0:T(128)S(1)}, u32[]{:S(2)}) copy-start(f32[128]{0:T(128)S(1)} %add_divide_fusion.1) | copy-start | bytes 1540
  138.1 25.5 %collective-permute-start.22 = (f32[128,256]{1,0:T(8,128)S(1)}, f32[128,256]{1,0:T(8,128)}, u32[]{:S(2)}, u32[]{:S(2)}) collective-permute-start(f32[128,256]{1,0:T(8,128)S(1)} %bitcast.548), channel_id=1, source_target_pairs={{0,12},{1,13},{2,14},{3,15},{4,0},{5,1},{6,2},{7,3},{8,4},{9,5},{1... | collective-permute-start | bytes 393224 | tf_op jit(solution)/shard_map/ppermute | solution.py:39
  181.1 6.5 %collective-permute-start.23 = (f32[1,128,256]{2,1,0:T(8,128)S(1)}, f32[1,128,256]{2,1,0:T(8,128)S(1)}, u32[]{:S(2)}, u32[]{:S(2)}) collective-permute-start(f32[1,128,256]{2,1,0:T(8,128)S(1)} %get-tuple-element.21), channel_id=1, source_target_pairs={{0,16},{16,0},{1,17},{17,1},{2,18},{18,2},{3,19},{19,3},{4,20},{20... | collective-permute-start | bytes 393224 | tf_op jit(solution)/shard_map/ppermute | solution.py:28
  183.1 12.3 %collective-permute-start.24 = (f32[1,128,256]{2,1,0:T(8,128)}, f32[1,128,256]{2,1,0:T(8,128)}, u32[]{:S(2)}, u32[]{:S(2)}) collective-permute-start(f32[1,128,256]{2,1,0:T(8,128)} %get-tuple-element.17), channel_id=1, source_target_pairs={{16,0},{0,16},{17,1},{1,17},{18,2},{2,18},{19,3},{3,19},{20,4},{4,... | collective-permute-start | bytes 393224 | tf_op jit(solution)/shard_map/ppermute | solution.py:31
  183.2 16.3 %collective-permute-start.25 = (f32[1,128,256]{2,1,0:T(8,128)}, f32[1,128,256]{2,1,0:T(8,128)}, u32[]{:S(2)}, u32[]{:S(2)}) collective-permute-start(f32[1,128,256]{2,1,0:T(8,128)} %get-tuple-element.20), channel_id=1, source_target_pairs={{0,1},{1,2},{2,3},{3,4},{4,5},{5,6},{6,7},{7,8},{8,9},{9,10},{10,1... | collective-permute-start | bytes 393224 | tf_op jit(solution)/shard_map/ppermute | solution.py:28
  183.2 20.3 %collective-permute-start.26 = (f32[1,128,256]{2,1,0:T(8,128)}, f32[1,128,256]{2,1,0:T(8,128)}, u32[]{:S(2)}, u32[]{:S(2)}) collective-permute-start(f32[1,128,256]{2,1,0:T(8,128)} %get-tuple-element.18), channel_id=1, source_target_pairs={{1,0},{2,1},{3,2},{4,3},{5,4},{6,5},{7,6},{8,7},{9,8},{10,9},{11,1... | collective-permute-start | bytes 393224 | tf_op jit(solution)/shard_map/ppermute | solution.py:31
  187.6 19.9 %collective-permute-start.27 = (f32[128,256]{1,0:T(8,128)}, f32[128,256]{1,0:T(8,128)}, u32[]{:S(2)}, u32[]{:S(2)}) collective-permute-start(f32[128,256]{1,0:T(8,128)} %get-tuple-element.19), channel_id=1, source_target_pairs={{0,4},{1,5},{2,6},{3,7},{4,8},{5,9},{6,10},{7,11},{8,12},{9,13},{1... | collective-permute-start | bytes 393224 | tf_op jit(solution)/shard_map/ppermute | solution.py:39
  187.6 26.0 %collective-permute-start.28 = (f32[128,256]{1,0:T(8,128)}, f32[128,256]{1,0:T(8,128)}, u32[]{:S(2)}, u32[]{:S(2)}) collective-permute-start(f32[128,256]{1,0:T(8,128)} %get-tuple-element.16), channel_id=1, source_target_pairs={{0,12},{1,13},{2,14},{3,15},{4,0},{5,1},{6,2},{7,3},{8,4},{9,5},{1... | collective-permute-start | bytes 393224 | tf_op jit(solution)/shard_map/ppermute | solution.py:39
  204.5 61.1 %copy-start.93 = (f32[128]{0:T(128)S(1)}, f32[128]{0:T(128)}, u32[]{:S(2)}) copy-start(f32[128]{0:T(128)} %get-tuple-element.9) | copy-start | bytes 1540
  217.0 50.1 %copy-start.46 = (f32[256,128]{0,1:T(8,128)}, f32[256,128]{0,1:T(8,128)S(1)}, u32[]{:S(2)}) copy-start(f32[256,128]{0,1:T(8,128)S(1)} %copy.134) | copy-start | bytes 393220
  228.7 42.2 %copy-start.90 = (s32[24]{0:T(128)S(1)}, s32[24]{0:T(128)}, u32[]{:S(2)}) copy-start(s32[24]{0:T(128)} %add.181) | copy-start | bytes 292
  228.7 85.9 %copy-start.86 = (f32[3,96]{1,0:T(4,128)S(1)}, f32[3,96]{1,0:T(4,128)}, u32[]{:S(2)}) copy-start(f32[3,96]{1,0:T(4,128)} %param.14) | copy-start | bytes 3460
  270.9 83.6 %copy-start.14 = (f32[128,1,256]{2,0,1:T(8,128)S(1)}, f32[128,1,256]{2,0,1:T(8,128)}, u32[]{:S(2)}) copy-start(f32[128,1,256]{2,0,1:T(8,128)} %copy-done.13) | copy-start | bytes 393220
  314.7 1.2 collective-permute-start.29
  315.9 3.9 %collective-permute-start.30 = (f32[128,6]{0,1:T(8,128)S(1)}, f32[128,6]{0,1:T(8,128)S(1)}, u32[]{:S(2)}, u32[]{:S(2)}) collective-permute-start(f32[128,6]{0,1:T(8,128)S(1)} %maximum_select_fusion.11), channel_id=1, source_target_pairs={{0,2},{1,3},{2,0},{3,1},{4,6},{5,7},{6,4},{7,5},{8,10},{9,11},{10,... | collective-permute-start | bytes 9224 | tf_op jit(solution)/shard_map/ppermute | solution.py:14
  319.8 3.7 collective-permute-start.31
  323.5 4.7 %collective-permute-start.32 = (f32[128,24]{0,1:T(8,128)S(1)}, f32[128,24]{0,1:T(8,128)S(1)}, u32[]{:S(2)}, u32[]{:S(2)}) collective-permute-start(f32[128,24]{0,1:T(8,128)S(1)} %maximum_select_fusion.7), channel_id=1, source_target_pairs={{0,8},{1,9},{2,10},{3,11},{4,12},{5,13},{6,14},{7,15},{8,0},{9,1},... | collective-permute-start | bytes 36872 | tf_op jit(solution)/shard_map/ppermute | solution.py:14
  328.2 3.8 collective-permute-start.33
  335.4 13.1 %collective-permute-start.34 = (f32[1,128,256]{2,1,0:T(8,128)S(1)}, f32[1,128,256]{2,1,0:T(8,128)S(1)}, u32[]{:S(2)}, u32[]{:S(2)}) collective-permute-start(f32[1,128,256]{2,1,0:T(8,128)S(1)} %bitcast.556), channel_id=1, source_target_pairs={{0,16},{16,0},{1,17},{17,1},{2,18},{18,2},{3,19},{19,3},{4,20},{20... | collective-permute-start | bytes 393224 | tf_op jit(solution)/shard_map/ppermute | solution.py:28
  338.4 18.2 %collective-permute-start.35 = (f32[1,128,256]{2,1,0:T(8,128)S(1)}, f32[1,128,256]{2,1,0:T(8,128)}, u32[]{:S(2)}, u32[]{:S(2)}) collective-permute-start(f32[1,128,256]{2,1,0:T(8,128)S(1)} %bitcast.557), channel_id=1, source_target_pairs={{16,0},{0,16},{17,1},{1,17},{18,2},{2,18},{19,3},{3,19},{20,4},{4,... | collective-permute-start | bytes 393224 | tf_op jit(solution)/shard_map/ppermute | solution.py:31
  339.5 19.8 %collective-permute-start.36 = (f32[1,128,256]{2,1,0:T(8,128)S(1)}, f32[1,128,256]{2,1,0:T(8,128)}, u32[]{:S(2)}, u32[]{:S(2)}) collective-permute-start(f32[1,128,256]{2,1,0:T(8,128)S(1)} %bitcast.554), channel_id=1, source_target_pairs={{0,1},{1,2},{2,3},{3,4},{4,5},{5,6},{6,7},{7,8},{8,9},{9,10},{10,1... | collective-permute-start | bytes 393224 | tf_op jit(solution)/shard_map/ppermute | solution.py:28
  340.6 21.4 %collective-permute-start.37 = (f32[1,128,256]{2,1,0:T(8,128)S(1)}, f32[1,128,256]{2,1,0:T(8,128)}, u32[]{:S(2)}, u32[]{:S(2)}) collective-permute-start(f32[1,128,256]{2,1,0:T(8,128)S(1)} %bitcast.555), channel_id=1, source_target_pairs={{1,0},{2,1},{3,2},{4,3},{5,4},{6,5},{7,6},{8,7},{9,8},{10,9},{11,1... | collective-permute-start | bytes 393224 | tf_op jit(solution)/shard_map/ppermute | solution.py:31
  346.1 18.5 %collective-permute-start.38 = (f32[128,256]{1,0:T(8,128)S(1)}, f32[128,256]{1,0:T(8,128)}, u32[]{:S(2)}, u32[]{:S(2)}) collective-permute-start(f32[128,256]{1,0:T(8,128)S(1)} %bitcast.553), channel_id=1, source_target_pairs={{0,4},{1,5},{2,6},{3,7},{4,8},{5,9},{6,10},{7,11},{8,12},{9,13},{1... | collective-permute-start | bytes 393224 | tf_op jit(solution)/shard_map/ppermute | solution.py:39
  348.4 18.9 %collective-permute-start.39 = (f32[128,256]{1,0:T(8,128)}, f32[128,256]{1,0:T(8,128)}, u32[]{:S(2)}, u32[]{:S(2)}) collective-permute-start(f32[128,256]{1,0:T(8,128)} %bitcast.149), channel_id=1, source_target_pairs={{0,12},{1,13},{2,14},{3,15},{4,0},{5,1},{6,2},{7,3},{8,4},{9,5},{1... | collective-permute-start | bytes 393224 | tf_op jit(solution)/shard_map/ppermute | solution.py:39
  (72 other events, 1038.5 us)
